TPU v7x, 32 devices: a whole 2x2x4 slice. The times are simulated.
32 devices in a mesh: row: 4 (over y, x), col: 2 (over core), vol: 4 (over z).
Axes of the slice: x: 2, y: 2, z: 4, core: 2. Of those that a mesh axis runs over, the one named last changes fastest.
Arguments:
- panel: bfloat16 [512, 131072], P('row', ('col', 'vol')), may hold values from -0.015625 to 0.015625
- density: float32 [32, 131072], P(None, ('col', 'vol')), may hold values from -6 to 6
- source: float32 [32, 32, 16, 512], P(None, 'row', 'col', 'vol'), may hold values from -6 to 6
- class_index: int32 [32, 16, 512], P('row', 'col', 'vol'), may hold values from 0 to 15
- class_values: float32 [16], replicated, may hold values from 0.2 to 5
- trace_count: int32 [4, 8], P('row'), may hold values from 1 to 64, 128 in all within a row
- trace_cell: int32 [4, 8, 64], P('row'), may hold values from 0 to 8191
Outputs:
- density_out: float32 [32, 131072], P(None, ('col', 'vol'))
- volume_out: float32 [32, 32, 16, 512], P(None, 'row', 'col', 'vol')
Inputs may be any that keep to these rules, and one draw needn't show every extreme that they name: `trace_count`: in each row r, the counts of the 8 blocks are 1 or more and sum to 128, so that every target of row tile r has exactly one live slot; the largest count of each row is 64. `trace_cell`: only the first trace_count[r, j] slots of block j are read; two slots may hit one cell.
All inputs are finite; a program needn't handle non-finite values.
Results may differ from a plain program's by a relative error of at most 0.00035.
Values may be sent and summed in bfloat16 or wider, within the bound.
No kernel may reach another device: no remote copies, remote signals or barrier semaphores. Data moves between devices by JAX's collectives and lax.ppermute only.
A program may use at most 128 MiB of HBM per device.

v0:
```python
import math
import jax
import jax.numpy as jnp
from jax import lax
from jax.sharding import PartitionSpec as P

SWEEPS = 4
OUTER = 2
MASS_TERM = 0.1
RELAXATION = 0.5
SPECTRUM_LOW = 0.1
SPECTRUM_HIGH = 2.0


def padded_2(value, sides, width):
    for axis, dim in sides:
        size, length = (lax.axis_size(axis), value.shape[dim])
        up = [(i, (i + 1) % size) for i in range(size - 1)]
        down = [(j, i) for i, j in up]
        last = lax.slice_in_dim(value, length - width, length, axis=dim)
        first = lax.slice_in_dim(value, 0, width, axis=dim)
        before = lax.ppermute(last, axis, up)
        after = lax.ppermute(first, axis, down)
        value = jnp.concatenate([before, value, after], axis=dim)
    return value


def relax_factors(count):
    middle = (SPECTRUM_HIGH + SPECTRUM_LOW) / 2.0
    spread = (SPECTRUM_HIGH - SPECTRUM_LOW) / 2.0
    return [
        1.0 / (middle + spread * math.cos(math.pi * (2 * order + 1) / (2 * count)))
        for order in range(count)
    ]


def neighbours(padded):
    center = padded[..., 1:-1, 1:-1, 1:-1]
    beside_all = padded[..., 2:, 1:-1, 1:-1] + padded[..., :-2, 1:-1, 1:-1]
    beside_all = beside_all + padded[..., 1:-1, 2:, 1:-1] + padded[..., 1:-1, :-2, 1:-1]
    beside_all = beside_all + padded[..., 1:-1, 1:-1, 2:] + padded[..., 1:-1, 1:-1, :-2]
    return (center, beside_all)


def local(panel, density, source, class_index, class_values, trace_count, trace_cell):
    factors = relax_factors(SWEEPS)
    classes = jnp.arange(class_values.shape[0], dtype=jnp.int32)
    conduct = jnp.sum(
        jnp.where(
            class_index[None] == classes[:, None, None, None],
            class_values[:, None, None, None],
            jnp.float32(0.0),
        ),
        axis=0,
    )
    diagonal = MASS_TERM + 6.0 * conduct
    counts = trace_count[0]
    block_index = lax.axis_index(("col", "vol"))
    offsets = jnp.cumsum(counts) - counts
    target_rows = panel.shape[0]
    slot_count = trace_cell.shape[2]
    slot_ids = jnp.arange(slot_count, dtype=jnp.int32)
    target_ids = jnp.arange(target_rows, dtype=jnp.int32)
    own_count = lax.dynamic_index_in_dim(counts, block_index, keepdims=False)
    first_target = lax.dynamic_index_in_dim(offsets, block_index, keepdims=False)
    cell_ids = lax.dynamic_index_in_dim(trace_cell[0], block_index, keepdims=False)
    live_slots = slot_ids < own_count
    select = (
        ((first_target + slot_ids)[:, None] == target_ids[None, :]) & live_slots[:, None]
    ).astype(jnp.float32)
    volume = jnp.zeros(source.shape, jnp.float32)
    field_shape = volume.shape
    share_width = density.shape[1] // lax.axis_size("row")
    share_state = lax.dynamic_slice_in_dim(
        density, lax.axis_index("row") * share_width, share_width, 1
    )
    rounded = density.astype(jnp.bfloat16)
    lead = field_shape[0]
    for iteration in range(OUTER):
        partial_value = lax.dot_general(
            rounded, panel, (((1,), (1,)), ((), ())), preferred_element_type=jnp.float32
        )
        potential = lax.psum(partial_value, ("col", "vol"))
        slot_values = jnp.dot(potential, select.T, precision=lax.Precision.HIGHEST)
        right_side = source.reshape(lead, -1).at[:, cell_ids].add(slot_values).reshape(field_shape)
        relax_volume = volume
        for factor in factors:
            padded = padded_2(relax_volume, (("row", 1), ("col", 2), ("vol", 3)), 1)
            center, beside_all = neighbours(padded)
            relax_volume = (
                center + factor * (right_side - diagonal * center + conduct * beside_all) / diagonal
            )
        volume = relax_volume
        mismatch = volume.reshape(lead, -1)[:, cell_ids] - slot_values
        own_fluxes = jnp.dot(mismatch, select, precision=lax.Precision.HIGHEST)
        fluxes = lax.psum(own_fluxes, ("col", "vol"))
        update = jnp.dot(fluxes.astype(jnp.bfloat16), panel, preferred_element_type=jnp.float32)
        share_state = share_state + RELAXATION * lax.psum_scatter(
            update, "row", scatter_dimension=1, tiled=True
        )
        if iteration + 1 < OUTER:
            rounded = lax.all_gather(share_state.astype(jnp.bfloat16), "row", axis=1, tiled=True)
    density = lax.all_gather(share_state, "row", axis=1, tiled=True)
    return (density, volume)


def solution(mesh):
    placed = (
        P("row", ("col", "vol")),
        P(None, ("col", "vol")),
        P(None, "row", "col", "vol"),
        P("row", "col", "vol"),
        P(),
        P("row", None),
        P("row", None, None),
    )
    return jax.shard_map(
        local,
        mesh=mesh,
        in_specs=placed,
        out_specs=(P(None, ("col", "vol")), P(None, "row", "col", "vol")),
        check_vma=False,
    )
```

profile of v0, /device:TPU:0, one launch (start us, length us, event | category | flops | bytes accessed | tf_op | source)
XLA Modules:
  0.0 584.9 jit_solution(7050335987216102525)
XLA Ops:
  8.5 5.5 collective-permute-start.1
  17.0 4.3 fusion.79
  22.7 28.9 %psum.28 = f32[32,128]{1,0:T(8,128)S(1)} all-reduce(f32[32,128]{1,0:T(8,128)S(1)} %fusion.79), channel_id=1, replica_groups=mesh['row'=4,'col'=2,'vol'=4] {'col','vol'}, use_global_device_ids=true, to_apply=%region_0.1 | all-reduce | flops 4096 | bytes 32768 | tf_op jit(solution)/shard_map/psum | solution.py:83
  53.7 3.2 collective-permute-start.3
  67.1 4.6 collective-permute-start.5
  75.2 4.5 copy.121
  79.6 5.0 scatter_fusion
  91.2 2.9 fusion.8
  95.4 5.0 collective-permute-start.7
  104.4 3.0 collective-permute-start.9
  117.0 4.6 collective-permute-start.11
  125.5 2.9 fusion.74
  129.7 5.2 collective-permute-start.13
  138.9 3.5 collective-permute-start.15
  150.7 5.0 collective-permute-start.17
  159.8 2.9 fusion.64
  164.1 5.9 %collective-permute-start.19 = (f32[32,1,8,128]{3,0,2,1:T(8,128)S(1)}, f32[32,1,8,128]{3,0,2,1:T(8,128)S(1)}, u32[]{:S(2)}, u32[]{:S(2)}) collective-permute-start(f32[32,1,8,128]{3,0,2,1:T(8,128)S(1)} %get-tuple-element.46), channel_id=1, source_target_pairs={{0,8},{8,16},{16,24},{1,9},{9,17},{17,25},{2,10},{10,18},{18,26},{... | collective-permute-start | bytes 393224 | tf_op jit(solution)/shard_map/ppermute | solution.py:22
  173.9 3.0 collective-permute-start.21
  187.1 4.9 collective-permute-start.23
  196.0 2.9 fusion.54
  204.7 29.4 %psum.29 = bf16[32,128]{1,0:T(8,128)(2,1)S(1)} all-reduce(f32[32,128]{1,0:T(8,128)S(1)} %fusion.87), channel_id=1, replica_groups=mesh['row'=4,'col'=2,'vol'=4] {'col','vol'}, use_global_device_ids=true, to_apply=%region_4.5 | all-reduce | flops 4096 | bytes 24576 | tf_op jit(solution)/shard_map/psum | solution.py:96
  234.1 4.2 fusion.122
  238.4 38.0 %reduce-scatter.3.cloned.1.call-done = f32[32,4096]{1,0:T(8,128)} async-done(((f32[32,16384]{1,0:T(8,128)}), f32[32,4096]{1,0:T(8,128)}) %reduce-scatter.3.cloned.1.call-update) | async-done | bytes 524304 | tf_op jit(solution)/shard_map/reduce_scatter | solution.py:98
  279.7 4.6 collective-permute-start.25
  288.1 3.0 collective-permute-start.27
  297.1 3.4 collective-permute-start.29
  306.2 3.0 collective-permute-done.28
  311.1 4.0 fusion.120
  315.1 27.5 %psum.30 = f32[32,128]{1,0:T(8,128)S(1)} all-reduce(f32[32,128]{1,0:T(8,128)S(1)} %fusion.120), channel_id=1, replica_groups=mesh['row'=4,'col'=2,'vol'=4] {'col','vol'}, use_global_device_ids=true, to_apply=%region_6.7 | all-reduce | flops 4096 | bytes 32768 | tf_op jit(solution)/shard_map/psum | solution.py:83
  342.9 5.0 scatter_fusion.1
  350.7 3.0 fusion.44
  355.0 6.1 %collective-permute-start.31 = (f32[32,1,8,128]{3,0,2,1:T(8,128)S(1)}, f32[32,1,8,128]{3,0,2,1:T(8,128)S(1)}, u32[]{:S(2)}, u32[]{:S(2)}) collective-permute-start(f32[32,1,8,128]{3,0,2,1:T(8,128)S(1)} %get-tuple-element.42), channel_id=1, source_target_pairs={{0,8},{8,16},{16,24},{1,9},{9,17},{17,25},{2,10},{10,18},{18,26},{... | collective-permute-start | bytes 393224 | tf_op jit(solution)/shard_map/ppermute | solution.py:22
  365.4 3.0 collective-permute-start.33
  378.1 4.6 collective-permute-start.35
  386.5 2.9 fusion.34
  390.8 5.9 %collective-permute-start.37 = (f32[32,1,8,128]{3,0,2,1:T(8,128)S(1)}, f32[32,1,8,128]{3,0,2,1:T(8,128)S(1)}, u32[]{:S(2)}, u32[]{:S(2)}) collective-permute-start(f32[32,1,8,128]{3,0,2,1:T(8,128)S(1)} %get-tuple-element.40), channel_id=1, source_target_pairs={{0,8},{8,16},{16,24},{1,9},{9,17},{17,25},{2,10},{10,18},{18,26},{... | collective-permute-start | bytes 393224 | tf_op jit(solution)/shard_map/ppermute | solution.py:22
  400.6 3.0 collective-permute-start.39
  412.4 5.0 collective-permute-start.41
  421.5 2.9 fusion.24
  425.8 5.9 %collective-permute-start.43 = (f32[32,1,8,128]{3,0,2,1:T(8,128)S(1)}, f32[32,1,8,128]{3,0,2,1:T(8,128)S(1)}, u32[]{:S(2)}, u32[]{:S(2)}) collective-permute-start(f32[32,1,8,128]{3,0,2,1:T(8,128)S(1)} %get-tuple-element.38), channel_id=1, source_target_pairs={{0,8},{8,16},{16,24},{1,9},{9,17},{17,25},{2,10},{10,18},{18,26},{... | collective-permute-start | bytes 393224 | tf_op jit(solution)/shard_map/ppermute | solution.py:22
  435.7 3.3 collective-permute-start.45
  448.3 4.9 collective-permute-start.47
  457.3 2.9 fusion.14
  466.0 29.4 %psum.31 = bf16[32,128]{1,0:T(8,128)(2,1)S(1)} all-reduce(f32[32,128]{1,0:T(8,128)S(1)} %fusion.83), channel_id=1, replica_groups=mesh['row'=4,'col'=2,'vol'=4] {'col','vol'}, use_global_device_ids=true, to_apply=%region_8.9 | all-reduce | flops 4096 | bytes 24576 | tf_op jit(solution)/shard_map/psum | solution.py:96
  495.3 4.2 fusion.121
  499.6 38.0 %reduce-scatter.5.cloned.1.call-done = f32[32,4096]{1,0:T(8,128)} async-done(((f32[32,16384]{1,0:T(8,128)}), f32[32,4096]{1,0:T(8,128)}) %reduce-scatter.5.cloned.1.call-update) | async-done | bytes 524304 | tf_op jit(solution)/shard_map/reduce_scatter | solution.py:98
  541.3 33.8 %all-gather.5.cloned.1.call-done = f32[32,16384]{1,0:T(8,128)} async-done(((f32[32,4096]{1,0:T(8,128)}), f32[32,16384]{1,0:T(8,128)}) %all-gather.5.cloned.1.call-update) | async-done | bytes 2097168 | tf_op jit(solution)/shard_map/all_gather | solution.py:103
  575.1 3.0 copy.123
  (223 shorter events, 178.0 us)
Async XLA Ops:
  7.2 269.2 %reduce-scatter.3.cloned.1.call-start = ((), (), s32[]{:S(2)}) async-start(), calls=%async_computation.2 | async-start | bytes 2621440 | tf_op jit(solution)/shard_map/reduce_scatter | solution.py:98
  7.2 45.0 %collective-permute-start = (f32[32,1,8,128]{3,0,2,1:T(8,128)S(1)}, f32[32,1,8,128]{3,0,2,1:T(8,128)S(1)}, u32[]{:S(2)}, u32[]{:S(2)}) collective-permute-start(f32[32,1,8,128]{3,0,2,1:T(8,128)S(1)} %broadcast.65), channel_id=1, source_target_pairs={{8,0},{16,8},{24,16},{9,1},{17,9},{25,17},{10,2},{18,10},{26,18},{... | collective-permute-start | bytes 393224 | tf_op jit(solution)/shard_map/ppermute | solution.py:23
  8.5 43.7 %collective-permute-start.1 = (f32[32,1,8,128]{3,0,2,1:T(8,128)S(1)}, f32[32,1,8,128]{3,0,2,1:T(8,128)S(1)}, u32[]{:S(2)}, u32[]{:S(2)}) collective-permute-start(f32[32,1,8,128]{3,0,2,1:T(8,128)S(1)} %broadcast.65), channel_id=1, source_target_pairs={{0,8},{8,16},{16,24},{1,9},{9,17},{17,25},{2,10},{10,18},{18,26},{... | collective-permute-start | bytes 393224 | tf_op jit(solution)/shard_map/ppermute | solution.py:22
  52.4 4.7 collective-permute-start.2
  53.7 4.2 collective-permute-start.3
  63.3 24.1 %collective-permute-start.4 = (f32[32,10,10,1]{0,2,3,1:T(8,128)S(1)}, f32[32,10,10,1]{0,2,3,1:T(8,128)S(1)}, u32[]{:S(2)}, u32[]{:S(2)}) collective-permute-start(f32[32,10,10,1]{0,2,3,1:T(8,128)S(1)} %copy.75), channel_id=1, source_target_pairs={{1,0},{2,1},{3,2},{5,4},{6,5},{7,6},{9,8},{10,9},{11,10},{13,12},{... | collective-permute-start | bytes 38408 | tf_op jit(solution)/shard_map/ppermute | solution.py:23
  67.1 22.3 %collective-permute-start.5 = (f32[32,10,10,1]{0,2,3,1:T(8,128)S(1)}, f32[32,10,10,1]{0,2,3,1:T(8,128)S(1)}, u32[]{:S(2)}, u32[]{:S(2)}) collective-permute-start(f32[32,10,10,1]{0,2,3,1:T(8,128)S(1)} %copy.77), channel_id=1, source_target_pairs={{0,1},{1,2},{2,3},{4,5},{5,6},{6,7},{8,9},{9,10},{10,11},{12,13},{... | collective-permute-start | bytes 38408 | tf_op jit(solution)/shard_map/ppermute | solution.py:22
  94.1 7.8 %collective-permute-start.6 = (f32[32,1,8,128]{3,0,2,1:T(8,128)S(1)}, f32[32,1,8,128]{3,0,2,1:T(8,128)S(1)}, u32[]{:S(2)}, u32[]{:S(2)}) collective-permute-start(f32[32,1,8,128]{3,0,2,1:T(8,128)S(1)} %get-tuple-element.51), channel_id=1, source_target_pairs={{8,0},{16,8},{24,16},{9,1},{17,9},{25,17},{10,2},{18,10},{26,18},{... | collective-permute-start | bytes 393224 | tf_op jit(solution)/shard_map/ppermute | solution.py:23
  95.4 7.7 %collective-permute-start.7 = (f32[32,1,8,128]{3,0,2,1:T(8,128)S(1)}, f32[32,1,8,128]{3,0,2,1:T(8,128)S(1)}, u32[]{:S(2)}, u32[]{:S(2)}) collective-permute-start(f32[32,1,8,128]{3,0,2,1:T(8,128)S(1)} %get-tuple-element.50), channel_id=1, source_target_pairs={{0,8},{8,16},{16,24},{1,9},{9,17},{17,25},{2,10},{10,18},{18,26},{... | collective-permute-start | bytes 393224 | tf_op jit(solution)/shard_map/ppermute | solution.py:22
  103.1 4.4 collective-permute-start.8
  113.3 8.3 %collective-permute-start.10 = (f32[32,10,10,1]{0,2,3,1:T(8,128)S(1)}, f32[32,10,10,1]{0,2,3,1:T(8,128)S(1)}, u32[]{:S(2)}, u32[]{:S(2)}) collective-permute-start(f32[32,10,10,1]{0,2,3,1:T(8,128)S(1)} %copy.80), channel_id=1, source_target_pairs={{1,0},{2,1},{3,2},{5,4},{6,5},{7,6},{9,8},{10,9},{11,10},{13,12},{... | collective-permute-start | bytes 38408 | tf_op jit(solution)/shard_map/ppermute | solution.py:23
  117.0 6.6 %collective-permute-start.11 = (f32[32,10,10,1]{0,2,3,1:T(8,128)S(1)}, f32[32,10,10,1]{0,2,3,1:T(8,128)S(1)}, u32[]{:S(2)}, u32[]{:S(2)}) collective-permute-start(f32[32,10,10,1]{0,2,3,1:T(8,128)S(1)} %copy.82), channel_id=1, source_target_pairs={{0,1},{1,2},{2,3},{4,5},{5,6},{6,7},{8,9},{9,10},{10,11},{12,13},{... | collective-permute-start | bytes 38408 | tf_op jit(solution)/shard_map/ppermute | solution.py:22
  128.4 7.9 %collective-permute-start.12 = (f32[32,1,8,128]{3,0,2,1:T(8,128)S(1)}, f32[32,1,8,128]{3,0,2,1:T(8,128)S(1)}, u32[]{:S(2)}, u32[]{:S(2)}) collective-permute-start(f32[32,1,8,128]{3,0,2,1:T(8,128)S(1)} %get-tuple-element.49), channel_id=1, source_target_pairs={{8,0},{16,8},{24,16},{9,1},{17,9},{25,17},{10,2},{18,10},{26,18},{... | collective-permute-start | bytes 393224 | tf_op jit(solution)/shard_map/ppermute | solution.py:23
  129.7 7.8 %collective-permute-start.13 = (f32[32,1,8,128]{3,0,2,1:T(8,128)S(1)}, f32[32,1,8,128]{3,0,2,1:T(8,128)S(1)}, u32[]{:S(2)}, u32[]{:S(2)}) collective-permute-start(f32[32,1,8,128]{3,0,2,1:T(8,128)S(1)} %get-tuple-element.48), channel_id=1, source_target_pairs={{0,8},{8,16},{16,24},{1,9},{9,17},{17,25},{2,10},{10,18},{18,26},{... | collective-permute-start | bytes 393224 | tf_op jit(solution)/shard_map/ppermute | solution.py:22
  137.6 4.8 collective-permute-start.14
  138.9 4.1 collective-permute-start.15
  148.4 7.3 %collective-permute-start.16 = (f32[32,10,10,1]{0,2,3,1:T(8,128)S(1)}, f32[32,10,10,1]{0,2,3,1:T(8,128)S(1)}, u32[]{:S(2)}, u32[]{:S(2)}) collective-permute-start(f32[32,10,10,1]{0,2,3,1:T(8,128)S(1)} %copy.85), channel_id=1, source_target_pairs={{1,0},{2,1},{3,2},{5,4},{6,5},{7,6},{9,8},{10,9},{11,10},{13,12},{... | collective-permute-start | bytes 38408 | tf_op jit(solution)/shard_map/ppermute | solution.py:23
  150.7 7.2 %collective-permute-start.17 = (f32[32,10,10,1]{0,2,3,1:T(8,128)S(1)}, f32[32,10,10,1]{0,2,3,1:T(8,128)S(1)}, u32[]{:S(2)}, u32[]{:S(2)}) collective-permute-start(f32[32,10,10,1]{0,2,3,1:T(8,128)S(1)} %copy.87), channel_id=1, source_target_pairs={{0,1},{1,2},{2,3},{4,5},{5,6},{6,7},{8,9},{9,10},{10,11},{12,13},{... | collective-permute-start | bytes 38408 | tf_op jit(solution)/shard_map/ppermute | solution.py:22
  162.8 8.7 %collective-permute-start.18 = (f32[32,1,8,128]{3,0,2,1:T(8,128)S(1)}, f32[32,1,8,128]{3,0,2,1:T(8,128)S(1)}, u32[]{:S(2)}, u32[]{:S(2)}) collective-permute-start(f32[32,1,8,128]{3,0,2,1:T(8,128)S(1)} %get-tuple-element.47), channel_id=1, source_target_pairs={{8,0},{16,8},{24,16},{9,1},{17,9},{25,17},{10,2},{18,10},{26,18},{... | collective-permute-start | bytes 393224 | tf_op jit(solution)/shard_map/ppermute | solution.py:23
  164.1 8.5 %collective-permute-start.19 = (f32[32,1,8,128]{3,0,2,1:T(8,128)S(1)}, f32[32,1,8,128]{3,0,2,1:T(8,128)S(1)}, u32[]{:S(2)}, u32[]{:S(2)}) collective-permute-start(f32[32,1,8,128]{3,0,2,1:T(8,128)S(1)} %get-tuple-element.46), channel_id=1, source_target_pairs={{0,8},{8,16},{16,24},{1,9},{9,17},{17,25},{2,10},{10,18},{18,26},{... | collective-permute-start | bytes 393224 | tf_op jit(solution)/shard_map/ppermute | solution.py:22
  172.6 4.4 collective-permute-start.20
  173.9 4.1 collective-permute-start.21
  183.3 8.6 %collective-permute-start.22 = (f32[32,10,10,1]{0,2,3,1:T(8,128)S(1)}, f32[32,10,10,1]{0,2,3,1:T(8,128)S(1)}, u32[]{:S(2)}, u32[]{:S(2)}) collective-permute-start(f32[32,10,10,1]{0,2,3,1:T(8,128)S(1)} %copy.90), channel_id=1, source_target_pairs={{1,0},{2,1},{3,2},{5,4},{6,5},{7,6},{9,8},{10,9},{11,10},{13,12},{... | collective-permute-start | bytes 38408 | tf_op jit(solution)/shard_map/ppermute | solution.py:23
  187.1 7.1 %collective-permute-start.23 = (f32[32,10,10,1]{0,2,3,1:T(8,128)S(1)}, f32[32,10,10,1]{0,2,3,1:T(8,128)S(1)}, u32[]{:S(2)}, u32[]{:S(2)}) collective-permute-start(f32[32,10,10,1]{0,2,3,1:T(8,128)S(1)} %copy.92), channel_id=1, source_target_pairs={{0,1},{1,2},{2,3},{4,5},{5,6},{6,7},{8,9},{9,10},{10,11},{12,13},{... | collective-permute-start | bytes 38408 | tf_op jit(solution)/shard_map/ppermute | solution.py:22
  238.3 72.8 %all-gather.3.cloned.1.call-start = ((), (), s32[]{:S(2)}) async-start(), calls=%async_computation.3 | async-start | bytes 1310720 | tf_op jit(solution)/shard_map/all_gather | solution.py:102
  278.4 259.3 %reduce-scatter.5.cloned.1.call-start = ((), (), s32[]{:S(2)}) async-start(), calls=%async_computation.4 | async-start | bytes 2621440 | tf_op jit(solution)/shard_map/reduce_scatter | solution.py:98
  278.4 7.0 %collective-permute-start.24 = (f32[32,1,8,128]{3,0,2,1:T(8,128)S(1)}, f32[32,1,8,128]{3,0,2,1:T(8,128)S(1)}, u32[]{:S(2)}, u32[]{:S(2)}) collective-permute-start(f32[32,1,8,128]{3,0,2,1:T(8,128)S(1)} %get-tuple-element.45), channel_id=1, source_target_pairs={{8,0},{16,8},{24,16},{9,1},{17,9},{25,17},{10,2},{18,10},{26,18},{... | collective-permute-start | bytes 393224 | tf_op jit(solution)/shard_map/ppermute | solution.py:23
  279.7 7.1 %collective-permute-start.25 = (f32[32,1,8,128]{3,0,2,1:T(8,128)S(1)}, f32[32,1,8,128]{3,0,2,1:T(8,128)S(1)}, u32[]{:S(2)}, u32[]{:S(2)}) collective-permute-start(f32[32,1,8,128]{3,0,2,1:T(8,128)S(1)} %get-tuple-element.44), channel_id=1, source_target_pairs={{0,8},{8,16},{16,24},{1,9},{9,17},{17,25},{2,10},{10,18},{18,26},{... | collective-permute-start | bytes 393224 | tf_op jit(solution)/shard_map/ppermute | solution.py:22
  286.8 4.4 collective-permute-start.26
  288.1 4.1 collective-permute-start.27
  297.1 7.3 %collective-permute-start.29 = (f32[32,10,10,1]{0,2,3,1:T(8,128)S(1)}, f32[32,10,10,1]{0,2,3,1:T(8,128)S(1)}, u32[]{:S(2)}, u32[]{:S(2)}) collective-permute-start(f32[32,10,10,1]{0,2,3,1:T(8,128)S(1)} %copy.100), channel_id=1, source_target_pairs={{0,1},{1,2},{2,3},{4,5},{5,6},{6,7},{8,9},{9,10},{10,11},{12,13},{... | collective-permute-start | bytes 38408 | tf_op jit(solution)/shard_map/ppermute | solution.py:22
  302.9 6.3 %collective-permute-start.28 = (f32[32,10,10,1]{0,2,3,1:T(8,128)S(1)}, f32[32,10,10,1]{0,2,3,1:T(8,128)S(1)}, u32[]{:S(2)}, u32[]{:S(2)}) collective-permute-start(f32[32,10,10,1]{0,2,3,1:T(8,128)S(1)} %copy.98), channel_id=1, source_target_pairs={{1,0},{2,1},{3,2},{5,4},{6,5},{7,6},{9,8},{10,9},{11,10},{13,12},{... | collective-permute-start | bytes 38408 | tf_op jit(solution)/shard_map/ppermute | solution.py:23
  353.7 9.2 %collective-permute-start.30 = (f32[32,1,8,128]{3,0,2,1:T(8,128)S(1)}, f32[32,1,8,128]{3,0,2,1:T(8,128)S(1)}, u32[]{:S(2)}, u32[]{:S(2)}) collective-permute-start(f32[32,1,8,128]{3,0,2,1:T(8,128)S(1)} %get-tuple-element.43), channel_id=1, source_target_pairs={{8,0},{16,8},{24,16},{9,1},{17,9},{25,17},{10,2},{18,10},{26,18},{... | collective-permute-start | bytes 393224 | tf_op jit(solution)/shard_map/ppermute | solution.py:23
  355.0 9.1 %collective-permute-start.31 = (f32[32,1,8,128]{3,0,2,1:T(8,128)S(1)}, f32[32,1,8,128]{3,0,2,1:T(8,128)S(1)}, u32[]{:S(2)}, u32[]{:S(2)}) collective-permute-start(f32[32,1,8,128]{3,0,2,1:T(8,128)S(1)} %get-tuple-element.42), channel_id=1, source_target_pairs={{0,8},{8,16},{16,24},{1,9},{9,17},{17,25},{2,10},{10,18},{18,26},{... | collective-permute-start | bytes 393224 | tf_op jit(solution)/shard_map/ppermute | solution.py:22
  364.1 4.4 collective-permute-start.32
  374.4 8.3 %collective-permute-start.34 = (f32[32,10,10,1]{0,2,3,1:T(8,128)S(1)}, f32[32,10,10,1]{0,2,3,1:T(8,128)S(1)}, u32[]{:S(2)}, u32[]{:S(2)}) collective-permute-start(f32[32,10,10,1]{0,2,3,1:T(8,128)S(1)} %copy.103), channel_id=1, source_target_pairs={{1,0},{2,1},{3,2},{5,4},{6,5},{7,6},{9,8},{10,9},{11,10},{13,12},{... | collective-permute-start | bytes 38408 | tf_op jit(solution)/shard_map/ppermute | solution.py:23
  378.1 6.6 %collective-permute-start.35 = (f32[32,10,10,1]{0,2,3,1:T(8,128)S(1)}, f32[32,10,10,1]{0,2,3,1:T(8,128)S(1)}, u32[]{:S(2)}, u32[]{:S(2)}) collective-permute-start(f32[32,10,10,1]{0,2,3,1:T(8,128)S(1)} %copy.105), channel_id=1, source_target_pairs={{0,1},{1,2},{2,3},{4,5},{5,6},{6,7},{8,9},{9,10},{10,11},{12,13},{... | collective-permute-start | bytes 38408 | tf_op jit(solution)/shard_map/ppermute | solution.py:22
  389.5 8.6 %collective-permute-start.36 = (f32[32,1,8,128]{3,0,2,1:T(8,128)S(1)}, f32[32,1,8,128]{3,0,2,1:T(8,128)S(1)}, u32[]{:S(2)}, u32[]{:S(2)}) collective-permute-start(f32[32,1,8,128]{3,0,2,1:T(8,128)S(1)} %get-tuple-element.41), channel_id=1, source_target_pairs={{8,0},{16,8},{24,16},{9,1},{17,9},{25,17},{10,2},{18,10},{26,18},{... | collective-permute-start | bytes 393224 | tf_op jit(solution)/shard_map/ppermute | solution.py:23
  390.8 8.4 %collective-permute-start.37 = (f32[32,1,8,128]{3,0,2,1:T(8,128)S(1)}, f32[32,1,8,128]{3,0,2,1:T(8,128)S(1)}, u32[]{:S(2)}, u32[]{:S(2)}) collective-permute-start(f32[32,1,8,128]{3,0,2,1:T(8,128)S(1)} %get-tuple-element.40), channel_id=1, source_target_pairs={{0,8},{8,16},{16,24},{1,9},{9,17},{17,25},{2,10},{10,18},{18,26},{... | collective-permute-start | bytes 393224 | tf_op jit(solution)/shard_map/ppermute | solution.py:22
  399.3 4.4 collective-permute-start.38
  410.1 7.4 %collective-permute-start.40 = (f32[32,10,10,1]{0,2,3,1:T(8,128)S(1)}, f32[32,10,10,1]{0,2,3,1:T(8,128)S(1)}, u32[]{:S(2)}, u32[]{:S(2)}) collective-permute-start(f32[32,10,10,1]{0,2,3,1:T(8,128)S(1)} %copy.108), channel_id=1, source_target_pairs={{1,0},{2,1},{3,2},{5,4},{6,5},{7,6},{9,8},{10,9},{11,10},{13,12},{... | collective-permute-start | bytes 38408 | tf_op jit(solution)/shard_map/ppermute | solution.py:23
  412.4 7.3 %collective-permute-start.41 = (f32[32,10,10,1]{0,2,3,1:T(8,128)S(1)}, f32[32,10,10,1]{0,2,3,1:T(8,128)S(1)}, u32[]{:S(2)}, u32[]{:S(2)}) collective-permute-start(f32[32,10,10,1]{0,2,3,1:T(8,128)S(1)} %copy.110), channel_id=1, source_target_pairs={{0,1},{1,2},{2,3},{4,5},{5,6},{6,7},{8,9},{9,10},{10,11},{12,13},{... | collective-permute-start | bytes 38408 | tf_op jit(solution)/shard_map/ppermute | solution.py:22
  424.5 8.7 %collective-permute-start.42 = (f32[32,1,8,128]{3,0,2,1:T(8,128)S(1)}, f32[32,1,8,128]{3,0,2,1:T(8,128)S(1)}, u32[]{:S(2)}, u32[]{:S(2)}) collective-permute-start(f32[32,1,8,128]{3,0,2,1:T(8,128)S(1)} %get-tuple-element.39), channel_id=1, source_target_pairs={{8,0},{16,8},{24,16},{9,1},{17,9},{25,17},{10,2},{18,10},{26,18},{... | collective-permute-start | bytes 393224 | tf_op jit(solution)/shard_map/ppermute | solution.py:23
  425.8 8.5 %collective-permute-start.43 = (f32[32,1,8,128]{3,0,2,1:T(8,128)S(1)}, f32[32,1,8,128]{3,0,2,1:T(8,128)S(1)}, u32[]{:S(2)}, u32[]{:S(2)}) collective-permute-start(f32[32,1,8,128]{3,0,2,1:T(8,128)S(1)} %get-tuple-element.38), channel_id=1, source_target_pairs={{0,8},{8,16},{16,24},{1,9},{9,17},{17,25},{2,10},{10,18},{18,26},{... | collective-permute-start | bytes 393224 | tf_op jit(solution)/shard_map/ppermute | solution.py:22
  434.4 4.6 collective-permute-start.44
  444.6 8.6 %collective-permute-start.46 = (f32[32,10,10,1]{0,2,3,1:T(8,128)S(1)}, f32[32,10,10,1]{0,2,3,1:T(8,128)S(1)}, u32[]{:S(2)}, u32[]{:S(2)}) collective-permute-start(f32[32,10,10,1]{0,2,3,1:T(8,128)S(1)} %copy.113), channel_id=1, source_target_pairs={{1,0},{2,1},{3,2},{5,4},{6,5},{7,6},{9,8},{10,9},{11,10},{13,12},{... | collective-permute-start | bytes 38408 | tf_op jit(solution)/shard_map/ppermute | solution.py:23
  448.3 7.1 %collective-permute-start.47 = (f32[32,10,10,1]{0,2,3,1:T(8,128)S(1)}, f32[32,10,10,1]{0,2,3,1:T(8,128)S(1)}, u32[]{:S(2)}, u32[]{:S(2)}) collective-permute-start(f32[32,10,10,1]{0,2,3,1:T(8,128)S(1)} %copy.115), channel_id=1, source_target_pairs={{0,1},{1,2},{2,3},{4,5},{5,6},{6,7},{8,9},{9,10},{10,11},{12,13},{... | collective-permute-start | bytes 38408 | tf_op jit(solution)/shard_map/ppermute | solution.py:22
  499.6 75.6 %all-gather.5.cloned.1.call-start = ((), (), s32[]{:S(2)}) async-start(), calls=%async_computation.5 | async-start | bytes 2621440 | tf_op jit(solution)/shard_map/all_gather | solution.py:103
  (29 other events, 156.9 us)
Sparse Core Ops, SparseCore 0:
  238.4 37.9 reduce-scatter.2
  278.8 26.9 all-gather.2
  499.7 37.9 reduce-scatter.4
  539.9 35.1 all-gather.4
where the time goes:
time: 595 us; the launch traced here: 585 us
  waiting for transfers between devices  140 us (24%)
  starting transfers between devices  137 us (23%)
  local copies, waits for them, and re-layouts  116 us (19%)
  blocking collectives  115 us (19%)
  other arithmetic  43.5 us (7%)
  matrix products  17.5 us (3%)
  between operations  15 us (3%)
    ppermute x24, starting transfers between devices, padded_2(): before = lax.ppermute(last, axis, up)  106 us
    reduce_scatter x2, waiting for transfers between devices, local(): lax.psum_scatter(update, 'row', scatter_dimension=1, tiled=True)  76.1 us
    psum x2, blocking collectives, local(): fluxes = lax.psum(own_fluxes, ('col', 'vol'))  58.7 us
    psum x2, blocking collectives, local(): potential = lax.psum(partial_value, ('col', 'vol'))  56.4 us
    slice x16, local copies, waits for them, and re-layouts, padded_2(): first = lax.slice_in_dim(value, 0, width, axis=dim)  37.9 us
    all_gather x1, waiting for transfers between devices, local(): density = lax.all_gather(share_state, 'row', axis=1, tiled=True)  33.8 us
    ppermute x24, starting transfers between devices, padded_2(): after = lax.ppermute(first, axis, down)  31.2 us
    add x7, other arithmetic, local(): center + factor * (right_side - diagonal * center + conduct * beside_all)...  20.6 us
  transfers between devices with their start and end apart: 52, of which 32 were waited for; matrix products, arithmetic and copies ran while one was open for 11% of the time, Pallas kernels for 0%

commit v1 on v0

--- a/solution.py
+++ b/solution.py
@@ -100,7 +100,12 @@
         )
         if iteration + 1 < OUTER:
             rounded = lax.all_gather(share_state.astype(jnp.bfloat16), "row", axis=1, tiled=True)
-    density = lax.all_gather(share_state, "row", axis=1, tiled=True)
+    ring = [share_state]
+    for hop in range(3):
+        ring.append(lax.ppermute(ring[-1], "row", [(dev, (dev + 1) % 4) for dev in range(4)]))
+    density = jnp.roll(
+        jnp.concatenate(ring[::-1], axis=1), (lax.axis_index("row") + 1) * ring[0].shape[1], axis=1
+    )
     return (density, volume)
 
 

time: 595 us -> 598 us (level)
    ppermute x0 -> x3, waiting for transfers between devices: none -> 37 us  [local(): lax.ppermute(ring[-1], 'row', [(dev, (dev + 1) % 4) for dev in range(4)])]
    all_gather x1 -> x0, waiting for transfers between devices: 33.8 us -> none  [local(): density = lax.all_gather(share_state, 'row', axis=1, tiled=True)]
    unnamed x54 -> x60, local copies, waits for them, and re-layouts: 13.8 us -> 11 us
  transfers between devices with their start and end apart: 52 -> 54, of which waited for: 32 -> 34; matrix products, arithmetic and copies ran while one was open for 11% -> 11% of each run, Pallas kernels for 0% -> 0%
where the time goes in v1:
time: 598 us; the launch traced here: 588 us
  waiting for transfers between devices  144 us (24%)
  starting transfers between devices  140 us (23%)
  local copies, waits for them, and re-layouts  115 us (19%)
  blocking collectives  115 us (19%)
  other arithmetic  42.7 us (7%)
  matrix products  17.5 us (3%)
  between operations  15.1 us (3%)
    ppermute x24, starting transfers between devices, padded_2(): before = lax.ppermute(last, axis, up)  106 us
    reduce_scatter x2, waiting for transfers between devices, local(): lax.psum_scatter(update, 'row', scatter_dimension=1, tiled=True)  76.1 us
    psum x2, blocking collectives, local(): fluxes = lax.psum(own_fluxes, ('col', 'vol'))  58.7 us
    psum x2, blocking collectives, local(): potential = lax.psum(partial_value, ('col', 'vol'))  56.4 us
    slice x16, local copies, waits for them, and re-layouts, padded_2(): first = lax.slice_in_dim(value, 0, width, axis=dim)  37.9 us
    ppermute x3, waiting for transfers between devices, local(): lax.ppermute(ring[-1], 'row', [(dev, (dev + 1) % 4) for dev in range(4)])  37 us
    ppermute x24, starting transfers between devices, padded_2(): after = lax.ppermute(first, axis, down)  31.2 us
    add x7, other arithmetic, local(): center + factor * (right_side - diagonal * center + conduct * beside_all)...  20.6 us
  transfers between devices with their start and end apart: 54, of which 34 were waited for; matrix products, arithmetic and copies ran while one was open for 11% of the time, Pallas kernels for 0%

profile of v1, /device:TPU:0, one launch (start us, length us, event | category | flops | bytes accessed | tf_op | source)
XLA Modules:
  0.0 588.2 jit_solution(12613226298876122367)
XLA Ops:
  8.5 5.5 collective-permute-start.1
  17.0 4.3 fusion.79
  22.7 28.9 %psum.28 = f32[32,128]{1,0:T(8,128)S(1)} all-reduce(f32[32,128]{1,0:T(8,128)S(1)} %fusion.79), channel_id=1, replica_groups=mesh['row'=4,'col'=2,'vol'=4] {'col','vol'}, use_global_device_ids=true, to_apply=%region_0.1 | all-reduce | flops 4096 | bytes 32768 | tf_op jit(solution)/shard_map/psum | solution.py:83
  53.7 3.2 collective-permute-start.3
  67.1 4.6 collective-permute-start.5
  75.2 4.5 copy.121
  79.6 5.0 scatter_fusion
  95.4 5.0 collective-permute-start.7
  104.4 3.0 collective-permute-start.9
  117.0 4.6 collective-permute-start.11
  125.5 2.9 fusion.74
  129.7 5.2 collective-permute-start.13
  138.9 3.5 collective-permute-start.15
  150.7 5.0 collective-permute-start.17
  159.8 2.9 fusion.64
  164.1 5.9 %collective-permute-start.19 = (f32[32,1,8,128]{3,0,2,1:T(8,128)S(1)}, f32[32,1,8,128]{3,0,2,1:T(8,128)S(1)}, u32[]{:S(2)}, u32[]{:S(2)}) collective-permute-start(f32[32,1,8,128]{3,0,2,1:T(8,128)S(1)} %get-tuple-element.46), channel_id=1, source_target_pairs={{0,8},{8,16},{16,24},{1,9},{9,17},{17,25},{2,10},{10,18},{18,26},{... | collective-permute-start | bytes 393224 | tf_op jit(solution)/shard_map/ppermute | solution.py:22
  173.9 3.0 collective-permute-start.21
  187.1 4.9 collective-permute-start.23
  196.0 2.9 fusion.54
  204.7 29.4 %psum.29 = bf16[32,128]{1,0:T(8,128)(2,1)S(1)} all-reduce(f32[32,128]{1,0:T(8,128)S(1)} %fusion.87), channel_id=1, replica_groups=mesh['row'=4,'col'=2,'vol'=4] {'col','vol'}, use_global_device_ids=true, to_apply=%region_4.5 | all-reduce | flops 4096 | bytes 24576 | tf_op jit(solution)/shard_map/psum | solution.py:96
  234.1 4.2 fusion.122
  238.4 38.0 %reduce-scatter.3.cloned.1.call-done = f32[32,4096]{1,0:T(8,128)} async-done(((f32[32,16384]{1,0:T(8,128)}), f32[32,4096]{1,0:T(8,128)}) %reduce-scatter.3.cloned.1.call-update) | async-done | bytes 524304 | tf_op jit(solution)/shard_map/reduce_scatter | solution.py:98
  279.7 4.6 collective-permute-start.25
  288.1 3.0 collective-permute-start.27
  297.1 3.4 collective-permute-start.29
  306.2 3.0 collective-permute-done.28
  311.1 4.0 fusion.120
  315.1 27.5 %psum.30 = f32[32,128]{1,0:T(8,128)S(1)} all-reduce(f32[32,128]{1,0:T(8,128)S(1)} %fusion.120), channel_id=1, replica_groups=mesh['row'=4,'col'=2,'vol'=4] {'col','vol'}, use_global_device_ids=true, to_apply=%region_6.7 | all-reduce | flops 4096 | bytes 32768 | tf_op jit(solution)/shard_map/psum | solution.py:83
  342.9 5.0 scatter_fusion.1
  350.7 3.0 fusion.44
  355.0 6.1 %collective-permute-start.31 = (f32[32,1,8,128]{3,0,2,1:T(8,128)S(1)}, f32[32,1,8,128]{3,0,2,1:T(8,128)S(1)}, u32[]{:S(2)}, u32[]{:S(2)}) collective-permute-start(f32[32,1,8,128]{3,0,2,1:T(8,128)S(1)} %get-tuple-element.42), channel_id=1, source_target_pairs={{0,8},{8,16},{16,24},{1,9},{9,17},{17,25},{2,10},{10,18},{18,26},{... | collective-permute-start | bytes 393224 | tf_op jit(solution)/shard_map/ppermute | solution.py:22
  365.4 3.0 collective-permute-start.33
  378.1 4.6 collective-permute-start.35
  386.5 2.9 fusion.34
  390.8 5.9 %collective-permute-start.37 = (f32[32,1,8,128]{3,0,2,1:T(8,128)S(1)}, f32[32,1,8,128]{3,0,2,1:T(8,128)S(1)}, u32[]{:S(2)}, u32[]{:S(2)}) collective-permute-start(f32[32,1,8,128]{3,0,2,1:T(8,128)S(1)} %get-tuple-element.40), channel_id=1, source_target_pairs={{0,8},{8,16},{16,24},{1,9},{9,17},{17,25},{2,10},{10,18},{18,26},{... | collective-permute-start | bytes 393224 | tf_op jit(solution)/shard_map/ppermute | solution.py:22
  400.6 3.0 collective-permute-start.39
  412.4 5.0 collective-permute-start.41
  421.5 2.9 fusion.24
  425.8 5.9 %collective-permute-start.43 = (f32[32,1,8,128]{3,0,2,1:T(8,128)S(1)}, f32[32,1,8,128]{3,0,2,1:T(8,128)S(1)}, u32[]{:S(2)}, u32[]{:S(2)}) collective-permute-start(f32[32,1,8,128]{3,0,2,1:T(8,128)S(1)} %get-tuple-element.38), channel_id=1, source_target_pairs={{0,8},{8,16},{16,24},{1,9},{9,17},{17,25},{2,10},{10,18},{18,26},{... | collective-permute-start | bytes 393224 | tf_op jit(solution)/shard_map/ppermute | solution.py:22
  435.7 3.3 collective-permute-start.45
  448.3 4.9 collective-permute-start.47
  457.3 2.9 fusion.14
  466.0 29.4 %psum.31 = bf16[32,128]{1,0:T(8,128)(2,1)S(1)} all-reduce(f32[32,128]{1,0:T(8,128)S(1)} %fusion.83), channel_id=1, replica_groups=mesh['row'=4,'col'=2,'vol'=4] {'col','vol'}, use_global_device_ids=true, to_apply=%region_8.9 | all-reduce | flops 4096 | bytes 24576 | tf_op jit(solution)/shard_map/psum | solution.py:96
  495.3 4.2 fusion.121
  499.6 38.1 %reduce-scatter.5.cloned.1.call-done = f32[32,4096]{1,0:T(8,128)} async-done(((f32[32,16384]{1,0:T(8,128)}), f32[32,4096]{1,0:T(8,128)}) %reduce-scatter.5.cloned.1.call-update) | async-done | bytes 524304 | tf_op jit(solution)/shard_map/reduce_scatter | solution.py:98
  540.4 12.9 %collective-permute-done.48 = f32[32,4096]{1,0:T(8,128)S(1)} collective-permute-done((f32[32,4096]{1,0:T(8,128)S(1)}, f32[32,4096]{1,0:T(8,128)S(1)}, u32[]{:S(2)}, u32[]{:S(2)}) %collective-permute-start.48) | collective-permute-done | bytes 524320 | tf_op jit(solution)/shard_map/ppermute | solution.py:105
  553.9 13.0 %collective-permute-done.49 = f32[32,4096]{1,0:T(8,128)S(1)} collective-permute-done((f32[32,4096]{1,0:T(8,128)S(1)}, f32[32,4096]{1,0:T(8,128)S(1)}, u32[]{:S(2)}, u32[]{:S(2)}) %collective-permute-start.49) | collective-permute-done | bytes 524320 | tf_op jit(solution)/shard_map/ppermute | solution.py:105
  568.5 11.1 %collective-permute-done.50 = f32[32,4096]{1,0:T(8,128)S(1)} collective-permute-done((f32[32,4096]{1,0:T(8,128)S(1)}, f32[32,4096]{1,0:T(8,128)S(1)}, u32[]{:S(2)}, u32[]{:S(2)}) %collective-permute-start.50) | collective-permute-done | bytes 524320 | tf_op jit(solution)/shard_map/ppermute | solution.py:105
  (234 shorter events, 183.9 us)
Async XLA Ops:
  7.2 269.2 %reduce-scatter.3.cloned.1.call-start = ((), (), s32[]{:S(2)}) async-start(), calls=%async_computation.2 | async-start | bytes 2621440 | tf_op jit(solution)/shard_map/reduce_scatter | solution.py:98
  7.2 45.0 %collective-permute-start = (f32[32,1,8,128]{3,0,2,1:T(8,128)S(1)}, f32[32,1,8,128]{3,0,2,1:T(8,128)S(1)}, u32[]{:S(2)}, u32[]{:S(2)}) collective-permute-start(f32[32,1,8,128]{3,0,2,1:T(8,128)S(1)} %broadcast.66), channel_id=1, source_target_pairs={{8,0},{16,8},{24,16},{9,1},{17,9},{25,17},{10,2},{18,10},{26,18},{... | collective-permute-start | bytes 393224 | tf_op jit(solution)/shard_map/ppermute | solution.py:23
  8.5 43.7 %collective-permute-start.1 = (f32[32,1,8,128]{3,0,2,1:T(8,128)S(1)}, f32[32,1,8,128]{3,0,2,1:T(8,128)S(1)}, u32[]{:S(2)}, u32[]{:S(2)}) collective-permute-start(f32[32,1,8,128]{3,0,2,1:T(8,128)S(1)} %broadcast.66), channel_id=1, source_target_pairs={{0,8},{8,16},{16,24},{1,9},{9,17},{17,25},{2,10},{10,18},{18,26},{... | collective-permute-start | bytes 393224 | tf_op jit(solution)/shard_map/ppermute | solution.py:22
  52.4 4.7 collective-permute-start.2
  53.7 4.2 collective-permute-start.3
  63.3 24.1 %collective-permute-start.4 = (f32[32,10,10,1]{0,2,3,1:T(8,128)S(1)}, f32[32,10,10,1]{0,2,3,1:T(8,128)S(1)}, u32[]{:S(2)}, u32[]{:S(2)}) collective-permute-start(f32[32,10,10,1]{0,2,3,1:T(8,128)S(1)} %copy.75), channel_id=1, source_target_pairs={{1,0},{2,1},{3,2},{5,4},{6,5},{7,6},{9,8},{10,9},{11,10},{13,12},{... | collective-permute-start | bytes 38408 | tf_op jit(solution)/shard_map/ppermute | solution.py:23
  67.1 22.3 %collective-permute-start.5 = (f32[32,10,10,1]{0,2,3,1:T(8,128)S(1)}, f32[32,10,10,1]{0,2,3,1:T(8,128)S(1)}, u32[]{:S(2)}, u32[]{:S(2)}) collective-permute-start(f32[32,10,10,1]{0,2,3,1:T(8,128)S(1)} %copy.77), channel_id=1, source_target_pairs={{0,1},{1,2},{2,3},{4,5},{5,6},{6,7},{8,9},{9,10},{10,11},{12,13},{... | collective-permute-start | bytes 38408 | tf_op jit(solution)/shard_map/ppermute | solution.py:22
  94.1 7.8 %collective-permute-start.6 = (f32[32,1,8,128]{3,0,2,1:T(8,128)S(1)}, f32[32,1,8,128]{3,0,2,1:T(8,128)S(1)}, u32[]{:S(2)}, u32[]{:S(2)}) collective-permute-start(f32[32,1,8,128]{3,0,2,1:T(8,128)S(1)} %get-tuple-element.51), channel_id=1, source_target_pairs={{8,0},{16,8},{24,16},{9,1},{17,9},{25,17},{10,2},{18,10},{26,18},{... | collective-permute-start | bytes 393224 | tf_op jit(solution)/shard_map/ppermute | solution.py:23
  95.4 7.7 %collective-permute-start.7 = (f32[32,1,8,128]{3,0,2,1:T(8,128)S(1)}, f32[32,1,8,128]{3,0,2,1:T(8,128)S(1)}, u32[]{:S(2)}, u32[]{:S(2)}) collective-permute-start(f32[32,1,8,128]{3,0,2,1:T(8,128)S(1)} %get-tuple-element.50), channel_id=1, source_target_pairs={{0,8},{8,16},{16,24},{1,9},{9,17},{17,25},{2,10},{10,18},{18,26},{... | collective-permute-start | bytes 393224 | tf_op jit(solution)/shard_map/ppermute | solution.py:22
  103.1 4.4 collective-permute-start.8
  113.3 8.3 %collective-permute-start.10 = (f32[32,10,10,1]{0,2,3,1:T(8,128)S(1)}, f32[32,10,10,1]{0,2,3,1:T(8,128)S(1)}, u32[]{:S(2)}, u32[]{:S(2)}) collective-permute-start(f32[32,10,10,1]{0,2,3,1:T(8,128)S(1)} %copy.80), channel_id=1, source_target_pairs={{1,0},{2,1},{3,2},{5,4},{6,5},{7,6},{9,8},{10,9},{11,10},{13,12},{... | collective-permute-start | bytes 38408 | tf_op jit(solution)/shard_map/ppermute | solution.py:23
  117.0 6.6 %collective-permute-start.11 = (f32[32,10,10,1]{0,2,3,1:T(8,128)S(1)}, f32[32,10,10,1]{0,2,3,1:T(8,128)S(1)}, u32[]{:S(2)}, u32[]{:S(2)}) collective-permute-start(f32[32,10,10,1]{0,2,3,1:T(8,128)S(1)} %copy.82), channel_id=1, source_target_pairs={{0,1},{1,2},{2,3},{4,5},{5,6},{6,7},{8,9},{9,10},{10,11},{12,13},{... | collective-permute-start | bytes 38408 | tf_op jit(solution)/shard_map/ppermute | solution.py:22
  128.4 7.9 %collective-permute-start.12 = (f32[32,1,8,128]{3,0,2,1:T(8,128)S(1)}, f32[32,1,8,128]{3,0,2,1:T(8,128)S(1)}, u32[]{:S(2)}, u32[]{:S(2)}) collective-permute-start(f32[32,1,8,128]{3,0,2,1:T(8,128)S(1)} %get-tuple-element.49), channel_id=1, source_target_pairs={{8,0},{16,8},{24,16},{9,1},{17,9},{25,17},{10,2},{18,10},{26,18},{... | collective-permute-start | bytes 393224 | tf_op jit(solution)/shard_map/ppermute | solution.py:23
  129.7 7.8 %collective-permute-start.13 = (f32[32,1,8,128]{3,0,2,1:T(8,128)S(1)}, f32[32,1,8,128]{3,0,2,1:T(8,128)S(1)}, u32[]{:S(2)}, u32[]{:S(2)}) collective-permute-start(f32[32,1,8,128]{3,0,2,1:T(8,128)S(1)} %get-tuple-element.48), channel_id=1, source_target_pairs={{0,8},{8,16},{16,24},{1,9},{9,17},{17,25},{2,10},{10,18},{18,26},{... | collective-permute-start | bytes 393224 | tf_op jit(solution)/shard_map/ppermute | solution.py:22
  137.6 4.8 collective-permute-start.14
  138.9 4.1 collective-permute-start.15
  148.4 7.3 %collective-permute-start.16 = (f32[32,10,10,1]{0,2,3,1:T(8,128)S(1)}, f32[32,10,10,1]{0,2,3,1:T(8,128)S(1)}, u32[]{:S(2)}, u32[]{:S(2)}) collective-permute-start(f32[32,10,10,1]{0,2,3,1:T(8,128)S(1)} %copy.85), channel_id=1, source_target_pairs={{1,0},{2,1},{3,2},{5,4},{6,5},{7,6},{9,8},{10,9},{11,10},{13,12},{... | collective-permute-start | bytes 38408 | tf_op jit(solution)/shard_map/ppermute | solution.py:23
  150.7 7.2 %collective-permute-start.17 = (f32[32,10,10,1]{0,2,3,1:T(8,128)S(1)}, f32[32,10,10,1]{0,2,3,1:T(8,128)S(1)}, u32[]{:S(2)}, u32[]{:S(2)}) collective-permute-start(f32[32,10,10,1]{0,2,3,1:T(8,128)S(1)} %copy.87), channel_id=1, source_target_pairs={{0,1},{1,2},{2,3},{4,5},{5,6},{6,7},{8,9},{9,10},{10,11},{12,13},{... | collective-permute-start | bytes 38408 | tf_op jit(solution)/shard_map/ppermute | solution.py:22
  162.8 8.7 %collective-permute-start.18 = (f32[32,1,8,128]{3,0,2,1:T(8,128)S(1)}, f32[32,1,8,128]{3,0,2,1:T(8,128)S(1)}, u32[]{:S(2)}, u32[]{:S(2)}) collective-permute-start(f32[32,1,8,128]{3,0,2,1:T(8,128)S(1)} %get-tuple-element.47), channel_id=1, source_target_pairs={{8,0},{16,8},{24,16},{9,1},{17,9},{25,17},{10,2},{18,10},{26,18},{... | collective-permute-start | bytes 393224 | tf_op jit(solution)/shard_map/ppermute | solution.py:23
  164.1 8.5 %collective-permute-start.19 = (f32[32,1,8,128]{3,0,2,1:T(8,128)S(1)}, f32[32,1,8,128]{3,0,2,1:T(8,128)S(1)}, u32[]{:S(2)}, u32[]{:S(2)}) collective-permute-start(f32[32,1,8,128]{3,0,2,1:T(8,128)S(1)} %get-tuple-element.46), channel_id=1, source_target_pairs={{0,8},{8,16},{16,24},{1,9},{9,17},{17,25},{2,10},{10,18},{18,26},{... | collective-permute-start | bytes 393224 | tf_op jit(solution)/shard_map/ppermute | solution.py:22
  172.6 4.4 collective-permute-start.20
  183.3 8.6 %collective-permute-start.22 = (f32[32,10,10,1]{0,2,3,1:T(8,128)S(1)}, f32[32,10,10,1]{0,2,3,1:T(8,128)S(1)}, u32[]{:S(2)}, u32[]{:S(2)}) collective-permute-start(f32[32,10,10,1]{0,2,3,1:T(8,128)S(1)} %copy.90), channel_id=1, source_target_pairs={{1,0},{2,1},{3,2},{5,4},{6,5},{7,6},{9,8},{10,9},{11,10},{13,12},{... | collective-permute-start | bytes 38408 | tf_op jit(solution)/shard_map/ppermute | solution.py:23
  187.1 7.1 %collective-permute-start.23 = (f32[32,10,10,1]{0,2,3,1:T(8,128)S(1)}, f32[32,10,10,1]{0,2,3,1:T(8,128)S(1)}, u32[]{:S(2)}, u32[]{:S(2)}) collective-permute-start(f32[32,10,10,1]{0,2,3,1:T(8,128)S(1)} %copy.92), channel_id=1, source_target_pairs={{0,1},{1,2},{2,3},{4,5},{5,6},{6,7},{8,9},{9,10},{10,11},{12,13},{... | collective-permute-start | bytes 38408 | tf_op jit(solution)/shard_map/ppermute | solution.py:22
  238.3 72.8 %all-gather.2.cloned.1.call-start = ((), (), s32[]{:S(2)}) async-start(), calls=%async_computation.3 | async-start | bytes 1310720 | tf_op jit(solution)/shard_map/all_gather | solution.py:102
  278.4 259.3 %reduce-scatter.5.cloned.1.call-start = ((), (), s32[]{:S(2)}) async-start(), calls=%async_computation.4 | async-start | bytes 2621440 | tf_op jit(solution)/shard_map/reduce_scatter | solution.py:98
  278.4 7.0 %collective-permute-start.24 = (f32[32,1,8,128]{3,0,2,1:T(8,128)S(1)}, f32[32,1,8,128]{3,0,2,1:T(8,128)S(1)}, u32[]{:S(2)}, u32[]{:S(2)}) collective-permute-start(f32[32,1,8,128]{3,0,2,1:T(8,128)S(1)} %get-tuple-element.45), channel_id=1, source_target_pairs={{8,0},{16,8},{24,16},{9,1},{17,9},{25,17},{10,2},{18,10},{26,18},{... | collective-permute-start | bytes 393224 | tf_op jit(solution)/shard_map/ppermute | solution.py:23
  279.7 7.1 %collective-permute-start.25 = (f32[32,1,8,128]{3,0,2,1:T(8,128)S(1)}, f32[32,1,8,128]{3,0,2,1:T(8,128)S(1)}, u32[]{:S(2)}, u32[]{:S(2)}) collective-permute-start(f32[32,1,8,128]{3,0,2,1:T(8,128)S(1)} %get-tuple-element.44), channel_id=1, source_target_pairs={{0,8},{8,16},{16,24},{1,9},{9,17},{17,25},{2,10},{10,18},{18,26},{... | collective-permute-start | bytes 393224 | tf_op jit(solution)/shard_map/ppermute | solution.py:22
  286.8 4.4 collective-permute-start.26
  297.1 7.3 %collective-permute-start.29 = (f32[32,10,10,1]{0,2,3,1:T(8,128)S(1)}, f32[32,10,10,1]{0,2,3,1:T(8,128)S(1)}, u32[]{:S(2)}, u32[]{:S(2)}) collective-permute-start(f32[32,10,10,1]{0,2,3,1:T(8,128)S(1)} %copy.100), channel_id=1, source_target_pairs={{0,1},{1,2},{2,3},{4,5},{5,6},{6,7},{8,9},{9,10},{10,11},{12,13},{... | collective-permute-start | bytes 38408 | tf_op jit(solution)/shard_map/ppermute | solution.py:22
  302.9 6.3 %collective-permute-start.28 = (f32[32,10,10,1]{0,2,3,1:T(8,128)S(1)}, f32[32,10,10,1]{0,2,3,1:T(8,128)S(1)}, u32[]{:S(2)}, u32[]{:S(2)}) collective-permute-start(f32[32,10,10,1]{0,2,3,1:T(8,128)S(1)} %copy.98), channel_id=1, source_target_pairs={{1,0},{2,1},{3,2},{5,4},{6,5},{7,6},{9,8},{10,9},{11,10},{13,12},{... | collective-permute-start | bytes 38408 | tf_op jit(solution)/shard_map/ppermute | solution.py:23
  353.7 9.2 %collective-permute-start.30 = (f32[32,1,8,128]{3,0,2,1:T(8,128)S(1)}, f32[32,1,8,128]{3,0,2,1:T(8,128)S(1)}, u32[]{:S(2)}, u32[]{:S(2)}) collective-permute-start(f32[32,1,8,128]{3,0,2,1:T(8,128)S(1)} %get-tuple-element.43), channel_id=1, source_target_pairs={{8,0},{16,8},{24,16},{9,1},{17,9},{25,17},{10,2},{18,10},{26,18},{... | collective-permute-start | bytes 393224 | tf_op jit(solution)/shard_map/ppermute | solution.py:23
  355.0 9.1 %collective-permute-start.31 = (f32[32,1,8,128]{3,0,2,1:T(8,128)S(1)}, f32[32,1,8,128]{3,0,2,1:T(8,128)S(1)}, u32[]{:S(2)}, u32[]{:S(2)}) collective-permute-start(f32[32,1,8,128]{3,0,2,1:T(8,128)S(1)} %get-tuple-element.42), channel_id=1, source_target_pairs={{0,8},{8,16},{16,24},{1,9},{9,17},{17,25},{2,10},{10,18},{18,26},{... | collective-permute-start | bytes 393224 | tf_op jit(solution)/shard_map/ppermute | solution.py:22
  364.1 4.4 collective-permute-start.32
  374.4 8.3 %collective-permute-start.34 = (f32[32,10,10,1]{0,2,3,1:T(8,128)S(1)}, f32[32,10,10,1]{0,2,3,1:T(8,128)S(1)}, u32[]{:S(2)}, u32[]{:S(2)}) collective-permute-start(f32[32,10,10,1]{0,2,3,1:T(8,128)S(1)} %copy.103), channel_id=1, source_target_pairs={{1,0},{2,1},{3,2},{5,4},{6,5},{7,6},{9,8},{10,9},{11,10},{13,12},{... | collective-permute-start | bytes 38408 | tf_op jit(solution)/shard_map/ppermute | solution.py:23
  378.1 6.6 %collective-permute-start.35 = (f32[32,10,10,1]{0,2,3,1:T(8,128)S(1)}, f32[32,10,10,1]{0,2,3,1:T(8,128)S(1)}, u32[]{:S(2)}, u32[]{:S(2)}) collective-permute-start(f32[32,10,10,1]{0,2,3,1:T(8,128)S(1)} %copy.105), channel_id=1, source_target_pairs={{0,1},{1,2},{2,3},{4,5},{5,6},{6,7},{8,9},{9,10},{10,11},{12,13},{... | collective-permute-start | bytes 38408 | tf_op jit(solution)/shard_map/ppermute | solution.py:22
  389.5 8.6 %collective-permute-start.36 = (f32[32,1,8,128]{3,0,2,1:T(8,128)S(1)}, f32[32,1,8,128]{3,0,2,1:T(8,128)S(1)}, u32[]{:S(2)}, u32[]{:S(2)}) collective-permute-start(f32[32,1,8,128]{3,0,2,1:T(8,128)S(1)} %get-tuple-element.41), channel_id=1, source_target_pairs={{8,0},{16,8},{24,16},{9,1},{17,9},{25,17},{10,2},{18,10},{26,18},{... | collective-permute-start | bytes 393224 | tf_op jit(solution)/shard_map/ppermute | solution.py:23
  390.8 8.4 %collective-permute-start.37 = (f32[32,1,8,128]{3,0,2,1:T(8,128)S(1)}, f32[32,1,8,128]{3,0,2,1:T(8,128)S(1)}, u32[]{:S(2)}, u32[]{:S(2)}) collective-permute-start(f32[32,1,8,128]{3,0,2,1:T(8,128)S(1)} %get-tuple-element.40), channel_id=1, source_target_pairs={{0,8},{8,16},{16,24},{1,9},{9,17},{17,25},{2,10},{10,18},{18,26},{... | collective-permute-start | bytes 393224 | tf_op jit(solution)/shard_map/ppermute | solution.py:22
  399.3 4.4 collective-permute-start.38
  410.1 7.4 %collective-permute-start.40 = (f32[32,10,10,1]{0,2,3,1:T(8,128)S(1)}, f32[32,10,10,1]{0,2,3,1:T(8,128)S(1)}, u32[]{:S(2)}, u32[]{:S(2)}) collective-permute-start(f32[32,10,10,1]{0,2,3,1:T(8,128)S(1)} %copy.108), channel_id=1, source_target_pairs={{1,0},{2,1},{3,2},{5,4},{6,5},{7,6},{9,8},{10,9},{11,10},{13,12},{... | collective-permute-start | bytes 38408 | tf_op jit(solution)/shard_map/ppermute | solution.py:23
  412.4 7.3 %collective-permute-start.41 = (f32[32,10,10,1]{0,2,3,1:T(8,128)S(1)}, f32[32,10,10,1]{0,2,3,1:T(8,128)S(1)}, u32[]{:S(2)}, u32[]{:S(2)}) collective-permute-start(f32[32,10,10,1]{0,2,3,1:T(8,128)S(1)} %copy.110), channel_id=1, source_target_pairs={{0,1},{1,2},{2,3},{4,5},{5,6},{6,7},{8,9},{9,10},{10,11},{12,13},{... | collective-permute-start | bytes 38408 | tf_op jit(solution)/shard_map/ppermute | solution.py:22
  424.5 8.7 %collective-permute-start.42 = (f32[32,1,8,128]{3,0,2,1:T(8,128)S(1)}, f32[32,1,8,128]{3,0,2,1:T(8,128)S(1)}, u32[]{:S(2)}, u32[]{:S(2)}) collective-permute-start(f32[32,1,8,128]{3,0,2,1:T(8,128)S(1)} %get-tuple-element.39), channel_id=1, source_target_pairs={{8,0},{16,8},{24,16},{9,1},{17,9},{25,17},{10,2},{18,10},{26,18},{... | collective-permute-start | bytes 393224 | tf_op jit(solution)/shard_map/ppermute | solution.py:23
  425.8 8.5 %collective-permute-start.43 = (f32[32,1,8,128]{3,0,2,1:T(8,128)S(1)}, f32[32,1,8,128]{3,0,2,1:T(8,128)S(1)}, u32[]{:S(2)}, u32[]{:S(2)}) collective-permute-start(f32[32,1,8,128]{3,0,2,1:T(8,128)S(1)} %get-tuple-element.38), channel_id=1, source_target_pairs={{0,8},{8,16},{16,24},{1,9},{9,17},{17,25},{2,10},{10,18},{18,26},{... | collective-permute-start | bytes 393224 | tf_op jit(solution)/shard_map/ppermute | solution.py:22
  434.4 4.6 collective-permute-start.44
  444.6 8.6 %collective-permute-start.46 = (f32[32,10,10,1]{0,2,3,1:T(8,128)S(1)}, f32[32,10,10,1]{0,2,3,1:T(8,128)S(1)}, u32[]{:S(2)}, u32[]{:S(2)}) collective-permute-start(f32[32,10,10,1]{0,2,3,1:T(8,128)S(1)} %copy.113), channel_id=1, source_target_pairs={{1,0},{2,1},{3,2},{5,4},{6,5},{7,6},{9,8},{10,9},{11,10},{13,12},{... | collective-permute-start | bytes 38408 | tf_op jit(solution)/shard_map/ppermute | solution.py:23
  448.3 7.1 %collective-permute-start.47 = (f32[32,10,10,1]{0,2,3,1:T(8,128)S(1)}, f32[32,10,10,1]{0,2,3,1:T(8,128)S(1)}, u32[]{:S(2)}, u32[]{:S(2)}) collective-permute-start(f32[32,10,10,1]{0,2,3,1:T(8,128)S(1)} %copy.115), channel_id=1, source_target_pairs={{0,1},{1,2},{2,3},{4,5},{5,6},{6,7},{8,9},{9,10},{10,11},{12,13},{... | collective-permute-start | bytes 38408 | tf_op jit(solution)/shard_map/ppermute | solution.py:22
  538.9 14.5 %collective-permute-start.48 = (f32[32,4096]{1,0:T(8,128)S(1)}, f32[32,4096]{1,0:T(8,128)S(1)}, u32[]{:S(2)}, u32[]{:S(2)}) collective-permute-start(f32[32,4096]{1,0:T(8,128)S(1)} %multiply_add_fusion), channel_id=1, source_target_pairs={{0,8},{8,16},{16,24},{24,0},{1,9},{9,17},{17,25},{25,1},{2,10},{10... | collective-permute-start | bytes 1572872 | tf_op jit(solution)/shard_map/ppermute | solution.py:105
  553.4 13.5 %collective-permute-start.49 = (f32[32,4096]{1,0:T(8,128)S(1)}, f32[32,4096]{1,0:T(8,128)S(1)}, u32[]{:S(2)}, u32[]{:S(2)}) collective-permute-start(f32[32,4096]{1,0:T(8,128)S(1)} %collective-permute-done.48), channel_id=1, source_target_pairs={{0,8},{8,16},{16,24},{24,0},{1,9},{9,17},{17,25},{25,1},{2,10},{10... | collective-permute-start | bytes 1572872 | tf_op jit(solution)/shard_map/ppermute | solution.py:105
  566.9 12.7 %collective-permute-start.50 = (f32[32,4096]{1,0:T(8,128)S(1)}, f32[32,4096]{1,0:T(8,128)S(1)}, u32[]{:S(2)}, u32[]{:S(2)}) collective-permute-start(f32[32,4096]{1,0:T(8,128)S(1)} %collective-permute-done.49), channel_id=1, source_target_pairs={{0,8},{8,16},{16,24},{24,0},{1,9},{9,17},{17,25},{25,1},{2,10},{10... | collective-permute-start | bytes 1572872 | tf_op jit(solution)/shard_map/ppermute | solution.py:105
  (31 other events, 165.0 us)
Sparse Core Ops, SparseCore 0:
  238.4 37.9 reduce-scatter.2
  278.8 26.9 all-gather.1
  499.7 37.9 reduce-scatter.4
